TPU v7x, 32 devices: a whole 2x2x4 slice. The times are simulated.
32 devices in a mesh: grp: 2 (over x), par: 8 (over z, y), ex: 2 (over core).
Axes of the slice: x: 2, y: 2, z: 4, core: 2. Of those that a mesh axis runs over, the one named last changes fastest.
Arguments:
- gradients: bfloat16 [512, 16384], P(('grp', 'ex'), 'par'), parts along dimension 0
- proj_seed: int32 [1], replicated, may hold values from 0 to 999999
- block_keys: int32 [1, 32], P(None, 'par'), may hold values from 0 to 999999
Outputs:
- features: bfloat16 [512, 8192], P(('grp', 'ex'), 'par'), parts along dimension 0
- kernel: float32 [512, 256], P(('grp', 'par'), 'ex'), parts along dimension 0
There are 2 independent parts, one for each index of `grp`. A program takes and returns all parts, laid end to end along the dimension named above; an argument that names none is the same for every part. Nothing has to cross between parts.
All inputs are finite; a program needn't handle non-finite values.
Results may differ from a plain program's by a relative error of at most 0.01.
Values may be sent and summed in bfloat16 or wider, within the bound.
A program may use at most 64 MiB of HBM per device.

v0:
```python
import math

import jax
import jax.numpy as jnp
from jax import lax
from jax.sharding import PartitionSpec as P

K = 8192
PBLK = 512


def rademacher(seed_value, block_key, row_index, col_index):
    mixed = row_index * 73856093 ^ col_index * 19349663 ^ block_key * 83492791 ^ seed_value
    mixed = mixed ^ mixed >> 13 & 524287
    mixed = mixed * 1540483477
    mixed = mixed ^ mixed >> 15 & 131071
    parity = mixed >> 11 & 1
    return (1 - 2 * parity).astype(jnp.bfloat16)


def project(slab, key_row, row_base, seed_value, col_index):
    block_count = slab.shape[1] // PBLK
    local_rows = jnp.arange(PBLK, dtype=jnp.int32)[:, None]
    summed = None
    for number in range(block_count):
        sign_block = rademacher(
            seed_value, key_row[number], row_base + number * PBLK + local_rows, col_index
        )
        slab_part = slab[:, number * PBLK : (number + 1) * PBLK]
        product = jnp.dot(slab_part, sign_block, preferred_element_type=jnp.float32)
        summed = product if summed is None else summed + product
    return summed


def local(gradients, proj_seed, block_keys):
    local_params = gradients.shape[1]
    shard_count = lax.axis_size("par")
    shard_index = lax.axis_index("par")
    seed_value = proj_seed[0]
    all_cols = jnp.arange(K, dtype=jnp.int32)[None, :]
    partial_value = project(
        gradients, block_keys[0], shard_index * local_params, seed_value, all_cols
    )
    projected = lax.psum_scatter(
        partial_value.astype(jnp.bfloat16), "par", scatter_dimension=1, tiled=True
    ).astype(jnp.float32)
    features = jnp.tanh(projected * (1.0 / math.sqrt(local_params * shard_count))).astype(
        jnp.bfloat16
    )
    gathered = lax.all_gather(features, "ex", axis=0, tiled=True)
    product = lax.dot_general(
        gathered, features, (((1,), (1,)), ((), ())), preferred_element_type=jnp.float32
    )
    kernel = lax.psum_scatter(
        (product * (1.0 / math.sqrt(K))).astype(jnp.bfloat16),
        "par",
        scatter_dimension=0,
        tiled=True,
    ).astype(jnp.float32)
    return (features, kernel)


def solution(mesh):
    placed = (P(("grp", "ex"), "par"), P(), P(None, "par"))
    return jax.shard_map(
        local,
        mesh=mesh,
        in_specs=placed,
        out_specs=(P(("grp", "ex"), "par"), P(("grp", "par"), "ex")),
        check_vma=False,
    )
```

profile of v0, /device:TPU:0, one launch (start us, length us, event | category | flops | bytes accessed | tf_op | source)
XLA Modules:
  0.0 190.4 jit_solution(15423520673000065363)
XLA Ops:
  7.2 0.0 reduce-scatter.3.cloned.1.call-start
  7.9 1.4 fusion.73
  11.8 0.0 copy-start
  11.8 8.7 %fusion.35 = f32[8192,128]{1,0:T(8,128)S(1)} fusion(s32[]{:T(128)} %bitcast.8, s32[]{:T(128)} %bitcast, s32[8192]{0:T(1024)S(1)} %iota_multiply_fusion, s32[512]{0:T(512)S(1)} %add_multiply_fusion.3, bf16[128,2048]{1,0:T(8,128)(2,1)} %param.3), kind=kOutput, calls=%fused_computation.42 | convolution fusion | flops 1136656384 | bytes 4361216 | tf_op jit(solution)/shard_map/dot_general | solution.py:30
  20.5 0.0 copy-done
  20.5 8.0 %convolution_add_fusion.2 = f32[8192,128]{1,0:T(8,128)S(1)} fusion(f32[8192,128]{1,0:T(8,128)S(1)} %fusion.35, s32[]{:T(128)} %bitcast.2, s32[512]{0:T(512)S(1)} %add_multiply_fusion.2, s32[]{:T(128)} %bitcast.11, s32[8192]{0:T(1024)S(1)} %iota_multiply_fusion, bf16[128,2048]{1,0:T(8,128)(2,1)S(1)} %copy-done), kind=kOutput, calls=%fused_computation.6 | convolution fusion | flops 1137704960 | bytes 8554504 | tf_op jit(solution)/shard_map/dot_general | solution.py:30
  28.5 8.1 %convolution_add_fusion.1 = f32[8192,128]{1,0:T(8,128)S(1)} fusion(f32[8192,128]{1,0:T(8,128)S(1)} %convolution_add_fusion.2, s32[]{:T(128)} %bitcast.3, s32[512]{0:T(512)S(1)} %add_multiply_fusion.1, s32[]{:T(128)} %bitcast.10, s32[8192]{0:T(1024)S(1)} %iota_multiply_fusion, bf16[128,2048]{1,0:T(8,128)(2,1)S(1)} %copy-done), kind=kOutput, calls=%fused_computation.5 | convolution fusion | flops 1137704960 | bytes 8554504 | tf_op jit(solution)/shard_map/dot_general | solution.py:30
  36.6 9.5 %fusion.1 = bf16[128,8192]{0,1:T(8,128)(2,1)} fusion(f32[8192,128]{1,0:T(8,128)S(1)} %convolution_add_fusion.1, s32[]{:T(128)} %bitcast.4, s32[512]{0:T(512)S(1)} %add_multiply_fusion, s32[]{:T(128)} %bitcast.9, s32[8192]{0:T(1024)S(1)} %iota_multiply_fusion, bf16[128,2048]{1,0:T(8,128)(2,1)S(1)} %copy-done), kind=kOutput, calls=%fused_computation.8 | convolution fusion | flops 1138753536 | bytes 6457352 | tf_op jit(solution)/shard_map/dot_general | solution.py:30
  46.1 0.0 reduce-scatter.3.cloned.1.call-update
  46.1 0.0 reduce-scatter.5.cloned.1.call-start
  46.2 70.6 %reduce-scatter.3.cloned.1.call-done = bf16[128,1024]{0,1:T(8,128)(2,1)} async-done(((bf16[128,8192]{0,1:T(8,128)(2,1)}), bf16[128,1024]{0,1:T(8,128)(2,1)}) %reduce-scatter.3.cloned.1.call-update) | async-done | bytes 262160 | tf_op jit(solution)/shard_map/reduce_scatter | solution.py:44
  116.8 1.0 tanh_convert_fusion
  117.8 2.2 %all_gather.3 = bf16[256,1024]{0,1:T(8,128)(2,1)S(1)} all-gather(bf16[128,1024]{0,1:T(8,128)(2,1)S(1)} %tanh_convert_fusion), channel_id=1, replica_groups=mesh['grp'=2,'par'=8,'ex'=2] {'ex'}, dimensions={0}, use_global_device_ids=true | all-gather | bytes 786432 | tf_op jit(solution)/shard_map/all_gather | solution.py:50
  120.0 1.9 fusion.36
  121.9 0.0 reduce-scatter.5.cloned.1.call-update
  121.9 0.9 copy.5
  122.8 59.5 %reduce-scatter.5.cloned.1.call-done = bf16[32,128]{1,0:T(8,128)(2,1)} async-done(((bf16[256,128]{1,0:T(8,128)(2,1)}), bf16[32,128]{1,0:T(8,128)(2,1)}) %reduce-scatter.5.cloned.1.call-update) | async-done | bytes 8208 | tf_op jit(solution)/shard_map/reduce_scatter | solution.py:54
  182.3 1.3 convert_element_type.39
  (5 shorter events, 0.0 us)
Async XLA Ops:
  7.2 109.6 %reduce-scatter.3.cloned.1.call-start = ((), (), s32[]{:S(2)}) async-start(), calls=%async_computation.2 | async-start | bytes 2359296 | tf_op jit(solution)/shard_map/reduce_scatter | solution.py:44
  11.8 8.7 %copy-start = (bf16[128,2048]{1,0:T(8,128)(2,1)S(1)}, bf16[128,2048]{1,0:T(8,128)(2,1)}, u32[]{:S(2)}) copy-start(bf16[128,2048]{1,0:T(8,128)(2,1)} %param.3) | copy-start | bytes 1572868
  46.1 136.2 %reduce-scatter.5.cloned.1.call-start = ((), (), s32[]{:S(2)}) async-start(), calls=%async_computation.3 | async-start | bytes 73728 | tf_op jit(solution)/shard_map/reduce_scatter | solution.py:54
Sparse Core Ops, SparseCore 0:
  46.2 70.5 reduce-scatter.2
  122.1 60.1 reduce-scatter.4
where the time goes:
time: 191 us; the launch traced here: 190 us
  waiting for transfers between devices  130 us (68%)
  matrix products  36.2 us (19%)
  between operations  17.2 us (9%)
  other arithmetic  2.36 us (1%)
  local copies, waits for them, and re-layouts  2.28 us (1%)
  blocking collectives  2.18 us (1%)
    reduce_scatter x1, waiting for transfers between devices, local(): lax.psum_scatter(partial_value.astype(jnp.bfloat16), 'par', scatter_dimen...  70.6 us
    reduce_scatter x1, waiting for transfers between devices, local(): lax.psum_scatter((product * (1.0 / math.sqrt(K))).astype(jnp.bfloat16), '...  59.5 us
    dot_general x4, matrix products, project(): product = jnp.dot(slab_part, sign_block, preferred_element_type=jnp.float32)  34.3 us
  transfers between devices with their start and end apart: 2, of which 2 were waited for; matrix products, arithmetic and copies ran while one was open for 0% of the time, Pallas kernels for 0%

commit v1 on v0

--- a/solution.py
+++ b/solution.py
@@ -1,12 +1,24 @@
+import functools
 import math
 
 import jax
 import jax.numpy as jnp
+import numpy as np
 from jax import lax
+from jax.experimental import pallas as pl
+from jax.experimental.pallas import tpu as pltpu
 from jax.sharding import PartitionSpec as P
 
 K = 8192
 PBLK = 512
+MESH = pl.DeviceIdType.MESH
+ROW_MUL = 73856093
+COL_MUL = 19349663
+KEY_MUL = 83492791
+MIX_MUL = int(np.array((1540483477 << 5) & 0xFFFFFFFF, np.uint32).astype(np.int32))
+
+NC = 2
+STEPS = 4
 
 
 def rademacher(seed_value, block_key, row_index, col_index):
@@ -32,7 +44,7 @@
     return summed
 
 
-def local(gradients, proj_seed, block_keys):
+def general(gradients, proj_seed, block_keys):
     local_params = gradients.shape[1]
     shard_count = lax.axis_size("par")
     shard_index = lax.axis_index("par")
@@ -60,10 +72,290 @@
     return (features, kernel)
 
 
+def fold(value):
+    return value ^ lax.shift_right_logical(value, 13)
+
+
+def line_kernel(
+    seed_ref, key_ref, g_ref, feat_ref, kern_ref,
+    x, signs, rows, keys, acc, outbox, inbox, feats, feats_in, kout, kin,
+    y_send, y_recv, c_send, c_recv, f_send, f_recv, key_sems,
+    z_send, z_recv, fx_send, fx_recv, k_send, k_recv,
+):
+    ex_rows, params = g_ref.shape
+    chunk = ex_rows // NC
+    width = K // 16
+    par, ex = lax.axis_index("par"), lax.axis_index("ex")
+    z, y = par // 2, par % 2
+    other_y, other_ex = 1 - y, 1 - ex
+    side = z // 2
+    is_end = jnp.logical_or(z == 0, z == 3)
+    is_mid = jnp.logical_not(is_end)
+    me = par * 2 + ex
+    blocks = params // PBLK
+
+    barrier = pltpu.get_barrier_semaphore()
+
+    def at_offset(k):
+        target = lax.rem(me + k, 16)
+        return {"par": target // 2, "ex": target % 2}
+
+    for k in range(1, 16):
+        pl.semaphore_signal(barrier, inc=1, device_id=at_offset(k), device_id_type=MESH)
+    pl.semaphore_wait(barrier, 15)
+
+    def remote(src, dst, send, recv, device):
+        return pltpu.make_async_remote_copy(
+            src_ref=src, dst_ref=dst, send_sem=send, recv_sem=recv,
+            device_id=device, device_id_type=MESH,
+        )
+
+    y_dev = {"par": z * 2 + other_y}
+    c_dev = {"ex": other_ex}
+    for b in range(blocks):
+        keys[y, b : b + 1, :] = jnp.full((1, 128), key_ref[0, b], jnp.int32)
+    key_copy = remote(keys.at[y], keys.at[y], key_sems.at[0], key_sems.at[1], y_dev)
+    key_copy.start()
+    y_copies, c_copies, f_copies = [], [], []
+    for c in range(NC):
+        part = g_ref.at[pl.ds(c * chunk, chunk)]
+        y_copies.append(remote(part, x.at[c, y, ex], y_send.at[c], y_recv.at[c], y_dev))
+        c_copies.append(remote(part, x.at[c, y, ex], c_send.at[c], c_recv.at[c], c_dev))
+        f_copies.append(
+            remote(
+                x.at[c, other_y, ex], x.at[c, other_y, ex], f_send.at[c], f_recv.at[c], c_dev
+            )
+        )
+        y_copies[c].start()
+    for c in range(NC):
+        c_copies[c].start()
+        x[c, y, ex] = g_ref[c * chunk : (c + 1) * chunk]
+
+    seed = seed_ref[0]
+
+    def make_rows(half):
+        for b in range(blocks):
+            index = lax.broadcasted_iota(jnp.int32, (PBLK, 128), 0)
+            index = index + ((z * 2 + half) * params + b * PBLK)
+            value = index * ROW_MUL ^ (keys[half, b : b + 1, :] * KEY_MUL ^ seed)
+            rows[half, b * PBLK : (b + 1) * PBLK, :] = fold(value)
+
+    def dest(step):
+        near = jnp.where(side == 0, z, 3 - z)
+        order = (3, 2, jnp.where(near == 0, 1, 0), near)[step]
+        return jnp.where(side == 0, order, 3 - order)
+
+    TILE = 64
+
+    def make_signs(step, half):
+        base = (dest(step) * 2 + y) * (2 * width) + ex * width
+        cols = []
+        for j in range(width // 128):
+            col = lax.broadcasted_iota(jnp.int32, (8, 128), 1) + (base + j * 128)
+            cols.append(fold(col * COL_MUL)[:1])
+
+        def body(i, carry):
+            start = pl.multiple_of(i * TILE, TILE)
+            row = rows[half, pl.ds(start, TILE), :]
+            for j, col in enumerate(cols):
+                mixed = (row ^ col) * MIX_MUL
+                mixed = mixed ^ (mixed << 15)
+                sign = jnp.where(mixed < 0, -1.0, 1.0).astype(jnp.bfloat16)
+                signs[step, half, pl.ds(start, TILE), j * 128 : (j + 1) * 128] = sign
+            return carry
+
+        lax.fori_loop(0, params // TILE, body, 0)
+
+    end_dev = {"par": (1 + side) * 2 + y}
+    far_dev = {"par": (3 - z) * 2 + y}
+    near_dev = {"par": (3 * side) * 2 + y}
+
+    def end_copy(c, s):
+        return remote(outbox.at[c, s], inbox.at[s, c], z_send.at[c, s], z_recv.at[s, c], end_dev)
+
+    def mid_copy(c, s):
+        slot = 3 + s
+        return remote(
+            outbox.at[c, s], inbox.at[slot, c], z_send.at[c, s], z_recv.at[slot, c],
+            far_dev if s < 2 else near_dev,
+        )
+
+    def arrived(slot, c):
+        remote(
+            inbox.at[slot, c], inbox.at[slot, c], z_send.at[c, 0], z_recv.at[slot, c], end_dev
+        ).wait_recv()
+
+    def multiply(c, s):
+        for n in range(width // 256):
+            cols = slice(n * 256, (n + 1) * 256)
+            total = None
+            for half in range(2):
+                left = x[c, half].reshape(2 * chunk, params)
+                product = jnp.dot(
+                    left, signs[s, half, :, cols], preferred_element_type=jnp.float32
+                )
+                total = product if total is None else total + product
+            acc[c, s, :, cols] = total
+        if s < 3:
+
+            @pl.when(is_end)
+            def _():
+                outbox[c, s] = acc[c, s].astype(jnp.bfloat16)
+                end_copy(c, s).start()
+
+    def finish(c, s):
+        @pl.when(is_mid)
+        def _():
+            slot = (0, 1, 3)[s]
+            arrived(slot, c)
+            outbox[c, s] = (acc[c, s] + inbox[slot, c].astype(jnp.float32)).astype(jnp.bfloat16)
+            mid_copy(c, s).start()
+
+    scale = 1.0 / math.sqrt(params * 8)
+
+    def fx_copy(c):
+        return remote(
+            feats.at[other_ex, pl.ds(c * chunk, chunk)], feats_in.at[pl.ds(c * chunk, chunk)],
+            fx_send.at[c], fx_recv.at[c], c_dev,
+        )
+
+    def settle(c):
+        @pl.when(is_mid)
+        def _():
+            arrived(2, c)
+            arrived(4, c)
+            acc[c, 3] += inbox[2, c].astype(jnp.float32) + inbox[4, c].astype(jnp.float32)
+
+        @pl.when(is_end)
+        def _():
+            arrived(5, c)
+            acc[c, 3] += inbox[5, c].astype(jnp.float32)
+
+        value = jnp.tanh(acc[c, 3] * scale).astype(jnp.bfloat16)
+        feats[:, c * chunk : (c + 1) * chunk, :] = value.reshape(2, chunk, width)
+        fx_copy(c).start()
+
+    def gathered(c):
+        c_copies[c].wait_recv()
+        f_copies[c].wait_recv()
+
+    make_rows(y)
+    make_signs(0, y)
+    key_copy.wait_recv()
+    make_rows(other_y)
+    make_signs(0, other_y)
+    y_copies[0].wait_recv()
+    f_copies[0].start()
+    gathered(0)
+    multiply(0, 0)
+    for s in (1, 2):
+        for half in range(2):
+            make_signs(s, half)
+        finish(0, s - 1)
+        multiply(0, s)
+    y_copies[1].wait_recv()
+    f_copies[1].start()
+    for half in range(2):
+        make_signs(3, half)
+    finish(0, 2)
+    gathered(1)
+    multiply(1, 0)
+    multiply(1, 1)
+    finish(1, 0)
+    multiply(1, 2)
+    finish(1, 1)
+    multiply(0, 3)
+    finish(1, 2)
+    settle(0)
+    multiply(1, 3)
+    settle(1)
+
+    whole = feats[...].reshape(2 * ex_rows, width)
+    product = lax.dot_general(
+        whole, whole, (((1,), (1,)), ((), ())), preferred_element_type=jnp.float32
+    ) * (1.0 / math.sqrt(K))
+    for half in range(2):
+        columns = product[:, half * 128 : (half + 1) * 128].astype(jnp.bfloat16)
+        kout[half] = columns.reshape(8, 32, 128)
+
+    def k_copy(k):
+        target = lax.rem(me + k, 16)
+        return remote(
+            kout.at[target % 2, target // 2], kin.at[k], k_send.at[k], k_recv.at[k], at_offset(k)
+        )
+
+    for k in range(1, 16):
+        k_copy(k).start()
+    feat_ref[:, pl.ds(pl.multiple_of(ex * width, width), width)] = feats[ex]
+    for c in range(NC):
+        fx_copy(c).wait_recv()
+    feat_ref[:, pl.ds(pl.multiple_of(other_ex * width, width), width)] = feats_in[...]
+    total = kout[ex, par].astype(jnp.float32)
+    for k in range(1, 16):
+        k_copy(k).wait_recv()
+        total += kin[k].astype(jnp.float32)
+    kern_ref[...] = total
+
+    key_copy.wait_send()
+    for c in range(NC):
+        y_copies[c].wait_send()
+        c_copies[c].wait_send()
+        f_copies[c].wait_send()
+        fx_copy(c).wait_send()
+        for s in range(3):
+            end_copy(c, s).wait_send()
+    for k in range(1, 16):
+        k_copy(k).wait_send()
+
+
+def line(gradients, proj_seed, block_keys):
+    ex_rows, params = gradients.shape
+    chunk = ex_rows // NC
+    width = K // 16
+    dma = pltpu.SemaphoreType.DMA
+    bf16 = jnp.bfloat16
+    return pl.pallas_call(
+        line_kernel,
+        out_shape=(
+            jax.ShapeDtypeStruct((ex_rows, K // 8), bf16),
+            jax.ShapeDtypeStruct((2 * ex_rows // 8, ex_rows), jnp.float32),
+        ),
+        in_specs=[
+            pl.BlockSpec(memory_space=pltpu.SMEM),
+            pl.BlockSpec(memory_space=pltpu.SMEM),
+            pl.BlockSpec(memory_space=pltpu.VMEM),
+        ],
+        out_specs=(
+            pl.BlockSpec(memory_space=pltpu.VMEM),
+            pl.BlockSpec(memory_space=pltpu.VMEM),
+        ),
+        scratch_shapes=[
+            pltpu.VMEM((NC, 2, 2, chunk, params), bf16),
+            pltpu.VMEM((STEPS, 2, params, width), bf16),
+            pltpu.VMEM((2, params, 128), jnp.int32),
+            pltpu.VMEM((2, 8, 128), jnp.int32),
+            pltpu.VMEM((NC, STEPS, 2 * chunk, width), jnp.float32),
+            pltpu.VMEM((NC, 3, 2 * chunk, width), bf16),
+            pltpu.VMEM((6, NC, 2 * chunk, width), bf16),
+            pltpu.VMEM((2, ex_rows, width), bf16),
+            pltpu.VMEM((ex_rows, width), bf16),
+            pltpu.VMEM((2, 8, 32, 128), bf16),
+            pltpu.VMEM((16, 32, 128), bf16),
+            dma((NC,)), dma((NC,)), dma((NC,)), dma((NC,)), dma((NC,)), dma((NC,)),
+            dma((2,)),
+            dma((NC, 3)), dma((6, NC)), dma((NC,)), dma((NC,)), dma((16,)), dma((16,)),
+        ],
+        compiler_params=pltpu.CompilerParams(
+            collective_id=0, has_side_effects=True, vmem_limit_bytes=56 * 1024 * 1024
+        ),
+    )(proj_seed, block_keys, gradients)
+
+
 def solution(mesh):
     placed = (P(("grp", "ex"), "par"), P(), P(None, "par"))
+    special = mesh.shape["par"] == 8 and mesh.shape["ex"] == 2
     return jax.shard_map(
-        local,
+        line if special else general,
         mesh=mesh,
         in_specs=placed,
         out_specs=(P(("grp", "ex"), "par"), P(("grp", "par"), "ex")),

time: 191 us -> 49.6 us (0.26)
  waiting for transfers between devices: 130 us -> 0 us
  Pallas kernels: 0 us -> 45.8 us
  matrix products: 36.2 us -> 0 us
  between operations: 17.2 us -> 1.29 us
  other arithmetic: 2.36 us -> 0 us
  blocking collectives: 2.18 us -> 0 us
    reduce_scatter x2 -> x0, waiting for transfers between devices: 130 us -> none  [the longest x1 70.6 us: local(): lax.psum_scatter(partial_value.astype(jnp.bfloat16), 'par', scatter_dimen...]
    pallas_call x0 -> x1, Pallas kernels: none -> 45.8 us  [line(): pl.pallas_call(line_kernel, out_shape=(jax.ShapeDtypeStruct((ex_rows, K /...]
    dot_general x5 -> x0, matrix products: 36.2 us -> none  [the longest x4 34.3 us: project(): product = jnp.dot(slab_part, sign_block, preferred_element_type=jnp.float32)]
    convert_element_type x2 -> x0, other arithmetic: 2.33 us -> none  [the longest x1 1.3 us: local(): kernel = lax.psum_scatter((product * (1.0 / math.sqrt(K))).astype(jnp.bfl...]
    all_gather x1 -> x0, blocking collectives: 2.18 us -> none  [local(): gathered = lax.all_gather(features, 'ex', axis=0, tiled=True)]
  transfers between devices with their start and end apart: 2 -> 0, of which waited for: 2 -> 0; matrix products, arithmetic and copies ran while one was open for 0% -> 0% of each run, Pallas kernels for 0% -> 0%
where the time goes in v1:
time: 49.6 us; the launch traced here: 49.4 us
  Pallas kernels  45.8 us (92%)
  local copies, waits for them, and re-layouts  2.28 us (5%)
  between operations  1.29 us (3%)
    pallas_call x1, Pallas kernels, line(): pl.pallas_call(line_kernel, out_shape=(jax.ShapeDtypeStruct((ex_rows, K /...  45.8 us
    unnamed x4, local copies, waits for them, and re-layouts  2.28 us

profile of v1, /device:TPU:0, one launch (start us, length us, event | category | flops | bytes accessed | tf_op | source)
XLA Modules:
  0.0 49.4 jit_solution(17897717932797867820)
XLA Ops:
  1.3 45.8 %shard_map.50 = (bf16[128,1024]{1,0:T(8,128)(2,1)}, f32[32,128]{1,0:T(8,128)}) custom-call(s32[1]{0:T(128)S(6)} %copy.7.seed_ref, s32[1,4]{1,0:T(1,128)} %key_ref.1, bf16[128,2048]{1,0:T(8,128)(2,1)} %g_ref.1), custom_call_target="tpu_custom_call" | custom-call | tf_op jit(solution)/shard_map/pallas_call | solution.py:317
  47.1 0.0 copy-start
  47.1 1.7 %copy.8 = bf16[128,1024]{1,0:T(8,128)(2,1)} copy(bf16[128,1024]{1,0:T(8,128)(2,1)} %get-tuple-element.4) | data formatting | bytes 524288
  48.8 0.0 copy-done
  48.8 0.6 %copy.9 = f32[32,128]{1,0:T(8,128)} copy(f32[32,128]{1,0:T(8,128)S(1)} %copy-done) | data formatting | bytes 32768
Async XLA Ops:
  47.1 1.7 %copy-start = (f32[32,128]{1,0:T(8,128)S(1)}, f32[32,128]{1,0:T(8,128)}, u32[]{:S(2)}) copy-start(f32[32,128]{1,0:T(8,128)} %get-tuple-element.5) | copy-start | bytes 49156

commit v2 on v1

--- a/solution.py
+++ b/solution.py
@@ -17,7 +17,7 @@
 KEY_MUL = 83492791
 MIX_MUL = int(np.array((1540483477 << 5) & 0xFFFFFFFF, np.uint32).astype(np.int32))
 
-NC = 2
+NC = 4
 STEPS = 4
 
 
@@ -102,7 +102,6 @@
 
     for k in range(1, 16):
         pl.semaphore_signal(barrier, inc=1, device_id=at_offset(k), device_id_type=MESH)
-    pl.semaphore_wait(barrier, 15)
 
     def remote(src, dst, send, recv, device):
         return pltpu.make_async_remote_copy(
@@ -114,23 +113,6 @@
     c_dev = {"ex": other_ex}
     for b in range(blocks):
         keys[y, b : b + 1, :] = jnp.full((1, 128), key_ref[0, b], jnp.int32)
-    key_copy = remote(keys.at[y], keys.at[y], key_sems.at[0], key_sems.at[1], y_dev)
-    key_copy.start()
-    y_copies, c_copies, f_copies = [], [], []
-    for c in range(NC):
-        part = g_ref.at[pl.ds(c * chunk, chunk)]
-        y_copies.append(remote(part, x.at[c, y, ex], y_send.at[c], y_recv.at[c], y_dev))
-        c_copies.append(remote(part, x.at[c, y, ex], c_send.at[c], c_recv.at[c], c_dev))
-        f_copies.append(
-            remote(
-                x.at[c, other_y, ex], x.at[c, other_y, ex], f_send.at[c], f_recv.at[c], c_dev
-            )
-        )
-        y_copies[c].start()
-    for c in range(NC):
-        c_copies[c].start()
-        x[c, y, ex] = g_ref[c * chunk : (c + 1) * chunk]
-
     seed = seed_ref[0]
 
     def make_rows(half):
@@ -185,30 +167,35 @@
             inbox.at[slot, c], inbox.at[slot, c], z_send.at[c, 0], z_recv.at[slot, c], end_dev
         ).wait_recv()
 
-    def multiply(c, s):
+    def multiply_own(s):
+        left = x[y].reshape(2 * ex_rows, params)
         for n in range(width // 256):
             cols = slice(n * 256, (n + 1) * 256)
-            total = None
-            for half in range(2):
-                left = x[c, half].reshape(2 * chunk, params)
-                product = jnp.dot(
-                    left, signs[s, half, :, cols], preferred_element_type=jnp.float32
-                )
-                total = product if total is None else total + product
-            acc[c, s, :, cols] = total
+            product = jnp.dot(left, signs[s, y, :, cols], preferred_element_type=jnp.float32)
+            acc[s, :, :, cols] = product.reshape(NC, 2 * chunk, 256)
+
+    def multiply(first, count, s):
+        left = x[other_y, first : first + count].reshape(count * 2 * chunk, params)
+        for n in range(width // 256):
+            cols = slice(n * 256, (n + 1) * 256)
+            product = jnp.dot(
+                left, signs[s, other_y, :, cols], preferred_element_type=jnp.float32
+            )
+            acc[s, first : first + count, :, cols] += product.reshape(count, 2 * chunk, 256)
         if s < 3:
 
             @pl.when(is_end)
             def _():
-                outbox[c, s] = acc[c, s].astype(jnp.bfloat16)
-                end_copy(c, s).start()
+                for c in range(first, first + count):
+                    outbox[c, s] = acc[s, c].astype(jnp.bfloat16)
+                    end_copy(c, s).start()
 
     def finish(c, s):
         @pl.when(is_mid)
         def _():
             slot = (0, 1, 3)[s]
             arrived(slot, c)
-            outbox[c, s] = (acc[c, s] + inbox[slot, c].astype(jnp.float32)).astype(jnp.bfloat16)
+            outbox[c, s] = (acc[s, c] + inbox[slot, c].astype(jnp.float32)).astype(jnp.bfloat16)
             mid_copy(c, s).start()
 
     scale = 1.0 / math.sqrt(params * 8)
@@ -224,51 +211,90 @@
         def _():
             arrived(2, c)
             arrived(4, c)
-            acc[c, 3] += inbox[2, c].astype(jnp.float32) + inbox[4, c].astype(jnp.float32)
+            acc[3, c] += inbox[2, c].astype(jnp.float32) + inbox[4, c].astype(jnp.float32)
 
         @pl.when(is_end)
         def _():
             arrived(5, c)
-            acc[c, 3] += inbox[5, c].astype(jnp.float32)
-
-        value = jnp.tanh(acc[c, 3] * scale).astype(jnp.bfloat16)
+            acc[3, c] += inbox[5, c].astype(jnp.float32)
+
+        value = jnp.tanh(acc[3, c] * scale).astype(jnp.bfloat16)
         feats[:, c * chunk : (c + 1) * chunk, :] = value.reshape(2, chunk, width)
         fx_copy(c).start()
 
-    def gathered(c):
-        c_copies[c].wait_recv()
-        f_copies[c].wait_recv()
+    def forward(c):
+        y_copies[c].wait_recv()
+        f_copies[c].start()
 
     make_rows(y)
-    make_signs(0, y)
+    for step in range(3):
+        make_signs(step, y)
+    for c in range(NC):
+        x[y, c, ex] = g_ref[c * chunk : (c + 1) * chunk]
+    pl.semaphore_wait(barrier, 15)
+
+    key_copy = remote(keys.at[y], keys.at[y], key_sems.at[0], key_sems.at[1], y_dev)
+    key_copy.start()
+    y_copies, c_copies, f_copies = [], [], []
+    for c in range(NC):
+        part = g_ref.at[pl.ds(c * chunk, chunk)]
+        y_copies.append(remote(part, x.at[y, c, ex], y_send.at[c], y_recv.at[c], y_dev))
+        c_copies.append(remote(part, x.at[y, c, ex], c_send.at[c], c_recv.at[c], c_dev))
+        f_copies.append(
+            remote(
+                x.at[other_y, c, ex], x.at[other_y, c, ex], f_send.at[c], f_recv.at[c], c_dev
+            )
+        )
+        y_copies[c].start()
+    for c in range(NC):
+        c_copies[c].start()
+
+    make_signs(3, y)
     key_copy.wait_recv()
     make_rows(other_y)
     make_signs(0, other_y)
-    y_copies[0].wait_recv()
-    f_copies[0].start()
-    gathered(0)
-    multiply(0, 0)
-    for s in (1, 2):
-        for half in range(2):
-            make_signs(s, half)
-        finish(0, s - 1)
-        multiply(0, s)
-    y_copies[1].wait_recv()
-    f_copies[1].start()
-    for half in range(2):
-        make_signs(3, half)
+    for c in range(NC):
+        c_copies[c].wait_recv()
+    multiply_own(0)
+    multiply_own(1)
+    forward(0)
+    make_signs(1, other_y)
+    f_copies[0].wait_recv()
+    multiply(0, 1, 0)
+    multiply(0, 1, 1)
+    forward(1)
+    make_signs(2, other_y)
+    f_copies[1].wait_recv()
+    multiply(1, 1, 0)
+    multiply(1, 1, 1)
+    finish(0, 0)
+    finish(0, 1)
+    forward(2)
+    multiply_own(2)
+    f_copies[2].wait_recv()
+    multiply(2, 1, 0)
+    multiply(2, 1, 1)
+    finish(1, 0)
+    finish(1, 1)
+    forward(3)
+    make_signs(3, other_y)
+    f_copies[3].wait_recv()
+    multiply(3, 1, 0)
+    multiply(3, 1, 1)
+    multiply(0, 2, 2)
+    finish(2, 0)
+    finish(2, 1)
     finish(0, 2)
-    gathered(1)
-    multiply(1, 0)
-    multiply(1, 1)
-    finish(1, 0)
-    multiply(1, 2)
-    finish(1, 1)
-    multiply(0, 3)
+    multiply(2, 2, 2)
+    finish(3, 0)
+    finish(3, 1)
     finish(1, 2)
-    settle(0)
-    multiply(1, 3)
-    settle(1)
+    finish(2, 2)
+    multiply_own(3)
+    multiply(0, NC, 3)
+    finish(3, 2)
+    for c in range(NC):
+        settle(c)
 
     whole = feats[...].reshape(2 * ex_rows, width)
     product = lax.dot_general(
@@ -308,13 +334,18 @@
         k_copy(k).wait_send()
 
 
+def write_kernel(feat_in, kern_in, feat_ref, kern_ref):
+    feat_ref[...] = feat_in[...]
+    kern_ref[...] = kern_in[...]
+
+
 def line(gradients, proj_seed, block_keys):
     ex_rows, params = gradients.shape
     chunk = ex_rows // NC
     width = K // 16
     dma = pltpu.SemaphoreType.DMA
     bf16 = jnp.bfloat16
-    return pl.pallas_call(
+    pair = pl.pallas_call(
         line_kernel,
         out_shape=(
             jax.ShapeDtypeStruct((ex_rows, K // 8), bf16),
@@ -330,11 +361,11 @@
             pl.BlockSpec(memory_space=pltpu.VMEM),
         ),
         scratch_shapes=[
-            pltpu.VMEM((NC, 2, 2, chunk, params), bf16),
+            pltpu.VMEM((2, NC, 2, chunk, params), bf16),
             pltpu.VMEM((STEPS, 2, params, width), bf16),
             pltpu.VMEM((2, params, 128), jnp.int32),
             pltpu.VMEM((2, 8, 128), jnp.int32),
-            pltpu.VMEM((NC, STEPS, 2 * chunk, width), jnp.float32),
+            pltpu.VMEM((STEPS, NC, 2 * chunk, width), jnp.float32),
             pltpu.VMEM((NC, 3, 2 * chunk, width), bf16),
             pltpu.VMEM((6, NC, 2 * chunk, width), bf16),
             pltpu.VMEM((2, ex_rows, width), bf16),
@@ -349,6 +380,10 @@
             collective_id=0, has_side_effects=True, vmem_limit_bytes=56 * 1024 * 1024
         ),
     )(proj_seed, block_keys, gradients)
+    return pl.pallas_call(
+        write_kernel,
+        out_shape=tuple(jax.ShapeDtypeStruct(part.shape, part.dtype) for part in pair),
+    )(*pair)
 
 
 def solution(mesh):

time: 49.6 us -> 44.2 us (0.89)
  Pallas kernels: 45.8 us -> 42.8 us
  local copies, waits for them, and re-layouts: 2.28 us -> 0 us
    pallas_call x1, Pallas kernels: 45.8 us -> 41.1 us  [line(): pl.pallas_call(line_kernel, out_shape=(jax.ShapeDtypeStruct((ex_rows, K /...]
    unnamed x4 -> x0, local copies, waits for them, and re-layouts: 2.28 us -> none
    pallas_call x0 -> x1, Pallas kernels: none -> 1.68 us  [line(): pl.pallas_call(write_kernel, out_shape=tuple((jax.ShapeDtypeStruct(part.s...]
where the time goes in v2:
time: 44.2 us; the launch traced here: 44.1 us
  Pallas kernels  42.8 us (97%)
  between operations  1.28 us (3%)
    pallas_call x1, Pallas kernels, line(): pl.pallas_call(line_kernel, out_shape=(jax.ShapeDtypeStruct((ex_rows, K /...  41.1 us
    pallas_call x1, Pallas kernels, line(): pl.pallas_call(write_kernel, out_shape=tuple((jax.ShapeDtypeStruct(part.s...  1.68 us

profile of v2, /device:TPU:0, one launch (start us, length us, event | category | flops | bytes accessed | tf_op | source)
XLA Modules:
  0.0 44.1 jit_solution(1652531647842514373)
XLA Ops:
  1.3 41.1 %shard_map.50 = (bf16[128,1024]{1,0:T(8,128)(2,1)}, f32[32,128]{1,0:T(8,128)}) custom-call(s32[1]{0:T(128)S(6)} %copy.5.seed_ref, s32[1,4]{1,0:T(1,128)} %key_ref.1, bf16[128,2048]{1,0:T(8,128)(2,1)} %g_ref.1), custom_call_target="tpu_custom_call" | custom-call | tf_op jit(solution)/shard_map/pallas_call | solution.py:348
  42.4 1.7 %shard_map.51 = (bf16[128,1024]{1,0:T(8,128)(2,1)}, f32[32,128]{1,0:T(8,128)}) custom-call(bf16[128,1024]{1,0:T(8,128)(2,1)} %get-tuple-element.4.feat_in, f32[32,128]{1,0:T(8,128)} %get-tuple-element.5.kern_in), custom_call_target="tpu_custom_call" | custom-call | tf_op jit(solution)/shard_map/pallas_call | solution.py:383

commit v3 on v2

--- a/solution.py
+++ b/solution.py
@@ -100,8 +100,22 @@
         target = lax.rem(me + k, 16)
         return {"par": target // 2, "ex": target % 2}
 
-    for k in range(1, 16):
-        pl.semaphore_signal(barrier, inc=1, device_id=at_offset(k), device_id_type=MESH)
+    y_dev = {"par": z * 2 + other_y}
+    c_dev = {"ex": other_ex}
+    end_dev = {"par": (1 + side) * 2 + y}
+    far_dev = {"par": (3 - z) * 2 + y}
+    near_dev = {"par": (3 * side) * 2 + y}
+    pl.semaphore_signal(barrier, inc=1, device_id=y_dev, device_id_type=MESH)
+    pl.semaphore_signal(barrier, inc=1, device_id=c_dev, device_id_type=MESH)
+
+    @pl.when(is_end)
+    def _():
+        pl.semaphore_signal(barrier, inc=1, device_id=end_dev, device_id_type=MESH)
+
+    @pl.when(is_mid)
+    def _():
+        pl.semaphore_signal(barrier, inc=1, device_id=far_dev, device_id_type=MESH)
+        pl.semaphore_signal(barrier, inc=1, device_id=near_dev, device_id_type=MESH)
 
     def remote(src, dst, send, recv, device):
         return pltpu.make_async_remote_copy(
@@ -109,8 +123,6 @@
             device_id=device, device_id_type=MESH,
         )
 
-    y_dev = {"par": z * 2 + other_y}
-    c_dev = {"ex": other_ex}
     for b in range(blocks):
         keys[y, b : b + 1, :] = jnp.full((1, 128), key_ref[0, b], jnp.int32)
     seed = seed_ref[0]
@@ -148,10 +160,6 @@
 
         lax.fori_loop(0, params // TILE, body, 0)
 
-    end_dev = {"par": (1 + side) * 2 + y}
-    far_dev = {"par": (3 - z) * 2 + y}
-    near_dev = {"par": (3 * side) * 2 + y}
-
     def end_copy(c, s):
         return remote(outbox.at[c, s], inbox.at[s, c], z_send.at[c, s], z_recv.at[s, c], end_dev)
 
@@ -231,7 +239,14 @@
         make_signs(step, y)
     for c in range(NC):
         x[y, c, ex] = g_ref[c * chunk : (c + 1) * chunk]
-    pl.semaphore_wait(barrier, 15)
+
+    @pl.when(is_end)
+    def _():
+        pl.semaphore_wait(barrier, 3)
+
+    @pl.when(is_mid)
+    def _():
+        pl.semaphore_wait(barrier, 4)
 
     key_copy = remote(keys.at[y], keys.at[y], key_sems.at[0], key_sems.at[1], y_dev)
     key_copy.start()
@@ -289,11 +304,12 @@
     finish(3, 0)
     finish(3, 1)
     finish(1, 2)
+    multiply_own(3)
     finish(2, 2)
-    multiply_own(3)
     multiply(0, NC, 3)
+    settle(0)
     finish(3, 2)
-    for c in range(NC):
+    for c in range(1, NC):
         settle(c)
 
     whole = feats[...].reshape(2 * ex_rows, width)

time: 44.2 us -> 44 us (level)
  no operation moved by 1% of the time
where the time goes in v3:
time: 44 us; the launch traced here: 43.9 us
  Pallas kernels  42.6 us (97%)
  between operations  1.28 us (3%)
    pallas_call x1, Pallas kernels, line(): pl.pallas_call(line_kernel, out_shape=(jax.ShapeDtypeStruct((ex_rows, K /...  40.9 us
    pallas_call x1, Pallas kernels, line(): pl.pallas_call(write_kernel, out_shape=tuple((jax.ShapeDtypeStruct(part.s...  1.68 us

profile of v3, /device:TPU:0, one launch (start us, length us, event | category | flops | bytes accessed | tf_op | source)
XLA Modules:
  0.0 43.9 jit_solution(7447962115409301798)
XLA Ops:
  1.3 40.9 %shard_map.50 = (bf16[128,1024]{1,0:T(8,128)(2,1)}, f32[32,128]{1,0:T(8,128)}) custom-call(s32[1]{0:T(128)S(6)} %copy.5.seed_ref, s32[1,4]{1,0:T(1,128)} %key_ref.1, bf16[128,2048]{1,0:T(8,128)(2,1)} %g_ref.1), custom_call_target="tpu_custom_call" | custom-call | tf_op jit(solution)/shard_map/pallas_call | solution.py:364
  42.2 1.7 %shard_map.51 = (bf16[128,1024]{1,0:T(8,128)(2,1)}, f32[32,128]{1,0:T(8,128)}) custom-call(bf16[128,1024]{1,0:T(8,128)(2,1)} %get-tuple-element.4.feat_in, f32[32,128]{1,0:T(8,128)} %get-tuple-element.5.kern_in), custom_call_target="tpu_custom_call" | custom-call | tf_op jit(solution)/shard_map/pallas_call | solution.py:399

commit v4 on v3

--- a/solution.py
+++ b/solution.py
@@ -234,12 +234,6 @@
         y_copies[c].wait_recv()
         f_copies[c].start()
 
-    make_rows(y)
-    for step in range(3):
-        make_signs(step, y)
-    for c in range(NC):
-        x[y, c, ex] = g_ref[c * chunk : (c + 1) * chunk]
-
     @pl.when(is_end)
     def _():
         pl.semaphore_wait(barrier, 3)
@@ -264,53 +258,60 @@
     for c in range(NC):
         c_copies[c].start()
 
-    make_signs(3, y)
+    for c in range(NC):
+        x[y, c, ex] = g_ref[c * chunk : (c + 1) * chunk]
+    make_rows(y)
+    make_signs(0, y)
+    make_signs(1, y)
     key_copy.wait_recv()
     make_rows(other_y)
     make_signs(0, other_y)
     for c in range(NC):
         c_copies[c].wait_recv()
     multiply_own(0)
-    multiply_own(1)
     forward(0)
     make_signs(1, other_y)
+    multiply_own(1)
     f_copies[0].wait_recv()
     multiply(0, 1, 0)
     multiply(0, 1, 1)
     forward(1)
-    make_signs(2, other_y)
+    make_signs(2, y)
     f_copies[1].wait_recv()
     multiply(1, 1, 0)
     multiply(1, 1, 1)
     finish(0, 0)
     finish(0, 1)
     forward(2)
-    multiply_own(2)
+    make_signs(2, other_y)
     f_copies[2].wait_recv()
     multiply(2, 1, 0)
     multiply(2, 1, 1)
     finish(1, 0)
     finish(1, 1)
     forward(3)
-    make_signs(3, other_y)
+    multiply_own(2)
     f_copies[3].wait_recv()
     multiply(3, 1, 0)
     multiply(3, 1, 1)
-    multiply(0, 2, 2)
     finish(2, 0)
     finish(2, 1)
+    multiply(0, 2, 2)
+    multiply(2, 2, 2)
     finish(0, 2)
-    multiply(2, 2, 2)
     finish(3, 0)
     finish(3, 1)
     finish(1, 2)
+    make_signs(3, y)
+    make_signs(3, other_y)
+    finish(2, 2)
     multiply_own(3)
-    finish(2, 2)
     multiply(0, NC, 3)
     settle(0)
+    settle(1)
     finish(3, 2)
-    for c in range(1, NC):
-        settle(c)
+    settle(2)
+    settle(3)
 
     whole = feats[...].reshape(2 * ex_rows, width)
     product = lax.dot_general(

time: 44 us -> 43.6 us (level)
  no operation moved by 1% of the time
where the time goes in v4:
time: 43.6 us; the launch traced here: 43.5 us
  Pallas kernels  42.2 us (97%)
  between operations  1.28 us (3%)
    pallas_call x1, Pallas kernels, line(): pl.pallas_call(line_kernel, out_shape=(jax.ShapeDtypeStruct((ex_rows, K /...  40.5 us
    pallas_call x1, Pallas kernels, line(): pl.pallas_call(write_kernel, out_shape=tuple((jax.ShapeDtypeStruct(part.s...  1.68 us

profile of v4, /device:TPU:0, one launch (start us, length us, event | category | flops | bytes accessed | tf_op | source)
XLA Modules:
  0.0 43.5 jit_solution(4072853637943874859)
XLA Ops:
  1.3 40.5 %shard_map.50 = (bf16[128,1024]{1,0:T(8,128)(2,1)}, f32[32,128]{1,0:T(8,128)}) custom-call(s32[1]{0:T(128)S(6)} %copy.5.seed_ref, s32[1,4]{1,0:T(1,128)} %key_ref.1, bf16[128,2048]{1,0:T(8,128)(2,1)} %g_ref.1), custom_call_target="tpu_custom_call" | custom-call | tf_op jit(solution)/shard_map/pallas_call | solution.py:365
  41.8 1.7 %shard_map.51 = (bf16[128,1024]{1,0:T(8,128)(2,1)}, f32[32,128]{1,0:T(8,128)}) custom-call(bf16[128,1024]{1,0:T(8,128)(2,1)} %get-tuple-element.4.feat_in, f32[32,128]{1,0:T(8,128)} %get-tuple-element.5.kern_in), custom_call_target="tpu_custom_call" | custom-call | tf_op jit(solution)/shard_map/pallas_call | solution.py:400
